TPU v7x, 32 devices: a whole 2x2x4 slice. The times are simulated.
32 devices in a mesh: batch: 8 (over z, core), vocab: 4 (over y, x).
Axes of the slice: x: 2, y: 2, z: 4, core: 2. Of those that a mesh axis runs over, the one named last changes fastest.
Arguments:
- hidden: bfloat16 [1024, 4096], P('batch'), may hold values from -40 to 40
- exit_layer: int32 [1024], P('batch'), may hold values from 0 to 7
- exit_gains: float32 [8, 4096], replicated, may hold values from 0.1 to 1.9
- unembed: bfloat16 [4096, 128256], P(None, ('batch', 'vocab')), may hold values from -10 to 10
- targets: int32 [1024], replicated, may hold values from 0 to 128255
- values: float32 [1024], P('batch'), may hold values from -6 to 6
- rewards: float32 [1024], P('batch'), may hold values from -2 to 2
- ref_logprob: float32 [1024], P('batch'), may hold values from -16 to -6
- segment_end: int32 [1024], P('batch'), may hold values 0 or 1
Outputs:
- logprob: float32 [1024], P('batch')
- advantages: float32 [1024], P('batch')
All inputs are finite; a program needn't handle non-finite values. No bound on the sum of `segment_end` on one device may be relied on, other than what follows from the above.
Results may differ from a plain program's by a relative error of at most 0.00054.
Values may be sent and summed in bfloat16 or wider, within the bound.
No kernel may reach another device: no remote copies, remote signals or barrier semaphores. Data moves between devices by JAX's collectives and lax.ppermute only.
A program may use at most 128 MiB of HBM per device.

v0:
```python
import jax
import jax.numpy as jnp
from jax import lax
from jax.sharding import PartitionSpec as P

epsilon_norm = 1e-05
discount = 1.0
trace_decay = 0.999
penalty_weight = 0.1


def joined(part, axis, combine):
    gathered = jax.tree.map(lambda a: lax.all_gather(a, axis), part)

    def take(source):
        return jax.tree.map(lambda a: lax.dynamic_index_in_dim(a, source, 0, False), gathered)

    return lax.fori_loop(
        1, lax.axis_size(axis), lambda source, state: combine(state, take(source)), take(0)
    )


def from_behind(value, axis, steps):
    count = lax.axis_size(axis)
    initial, last = (max(0, -steps), min(count, count - steps))
    return lax.ppermute(value, axis, [(source, source + steps) for source in range(initial, last)])


def normalize(rows, layers, exit_gains):
    states = rows.astype(jnp.float32)
    inverse = lax.rsqrt(jnp.mean(states * states, axis=-1, keepdims=True) + epsilon_norm)
    selector = (
        layers[:, None] == jnp.arange(exit_gains.shape[0], dtype=jnp.int32)[None, :]
    ).astype(jnp.float32)
    scaling = jnp.dot(selector, exit_gains, precision=lax.Precision.HIGHEST)
    return (states * inverse * scaling).astype(jnp.bfloat16)


def per_device(
    hidden, exit_layer, exit_gains, unembed, targets, values, rewards, ref_logprob, segment_end
):
    column_count = unembed.shape[1]
    column_start = lax.axis_index(("batch", "vocab")) * column_count
    columns = jnp.arange(column_count, dtype=jnp.int32)
    total_rows = targets.shape[0]
    owned = hidden.shape[0]
    peers = lax.axis_size("batch")
    width = hidden.shape[1]
    normed = normalize(hidden, exit_layer, exit_gains)
    gathered = lax.all_gather(normed, "batch", axis=0, tiled=True)
    block_rows = 512
    block_count = total_rows // block_rows

    def score_block(pair):
        rows_block, ids_block = pair
        logits = jnp.dot(rows_block, unembed, preferred_element_type=jnp.float32)
        row_max = jnp.max(logits, axis=1)
        row_total = jnp.sum(jnp.exp(logits - row_max[:, None]), axis=1)
        wanted = ids_block - column_start
        picked = jnp.sum(jnp.where(columns[None, :] == wanted[:, None], logits, 0.0), axis=1)
        return (row_max, row_total, picked)

    maxima, totals, picks = lax.map(
        score_block,
        (
            gathered.reshape(block_count, block_rows, width),
            targets.reshape(block_count, block_rows),
        ),
    )
    maxima = maxima.reshape(total_rows)
    totals = totals.reshape(total_rows)
    picks = picks.reshape(total_rows)
    maxima, totals, picks = (
        lax.all_to_all(maxima, "batch", split_axis=0, concat_axis=0, tiled=True),
        lax.all_to_all(totals, "batch", split_axis=0, concat_axis=0, tiled=True),
        lax.all_to_all(picks, "batch", split_axis=0, concat_axis=0, tiled=True),
    )
    maxima = maxima.reshape(peers, owned)
    totals = totals.reshape(peers, owned)
    picks = picks.reshape(peers, owned)
    group_max = jnp.max(maxima, axis=0)
    group_total = jnp.sum(totals * jnp.exp(maxima - group_max[None, :]), axis=0)
    group_pick = jnp.sum(picks, axis=0)

    def combine_groups(first, second):
        larger = jnp.maximum(first[0], second[0])
        summed = first[1] * jnp.exp(first[0] - larger) + second[1] * jnp.exp(second[0] - larger)
        return (larger, summed, first[2] + second[2])

    overall_max, overall_total, overall_pick = joined(
        (group_max, group_total, group_pick), "vocab", combine_groups
    )
    logprob = overall_pick - (overall_max + jnp.log(overall_total))
    following = from_behind(values[:1], "batch", -1)
    next_values = jnp.concatenate([values[1:], following])
    keeping = 1.0 - segment_end.astype(jnp.float32)
    shaped = rewards - penalty_weight * (logprob - ref_logprob)
    deltas = shaped + discount * next_values * keeping - values
    factors = discount * trace_decay * keeping

    def backward(running, inputs):
        factor, delta = inputs
        accrued = delta + factor * running[0]
        product = factor * running[1]
        return ((accrued, product), (accrued, product))

    finished, outputs = lax.scan(
        backward,
        (jnp.zeros((), jnp.float32), jnp.ones((), jnp.float32)),
        (factors, deltas),
        reverse=True,
    )
    local_adv, products = outputs
    head_adv = local_adv[:1]
    head_prod = products[:1]

    def relay_step(index, inbound):
        return from_behind(head_adv + head_prod * inbound, "batch", -1)

    incoming = lax.fori_loop(0, peers - 1, relay_step, jnp.zeros((1,), jnp.float32))
    advantages = local_adv + products * incoming
    return (logprob, advantages)


def solution(mesh):
    placed = (
        P("batch", None),
        P("batch"),
        P(),
        P(None, ("batch", "vocab")),
        P(),
        P("batch"),
        P("batch"),
        P("batch"),
        P("batch"),
    )
    return jax.shard_map(
        per_device, mesh=mesh, in_specs=placed, out_specs=(P("batch"), P("batch")), check_vma=False
    )
```

profile of v0, /device:TPU:1, one launch (start us, length us, event | category | flops | bytes accessed | tf_op | source)
XLA Modules:
  0.0 659.9 jit_solution(1969965212118673331)
XLA Ops:
  8.8 3.4 fusion.13
  12.9 83.9 %all-gather.8.cloned.1.call-done = bf16[1024,4096]{1,0:T(8,128)(2,1)} async-done(((bf16[128,4096]{1,0:T(8,128)(2,1)}), bf16[1024,4096]{1,0:T(8,128)(2,1)}) %all-gather.8.cloned.1.call-update) | async-done | bytes 8388624 | tf_op jit(solution)/shard_map/all_gather | solution.py:50
  96.8 49.9 %while.67 = (s32[]{:T(128)}, f32[2,512]{1,0:T(2,128)S(1)}, f32[2,512]{1,0:T(2,128)S(1)}, f32[2,512]{1,0:T(2,128)S(1)}, bf16[2,512,4096]{2,1,0:T(8,128)(2,1)}, /*...) while((s32[]{:T(128)}, f32[2,512]{1,0:T(2,128)S(1)}, ...), condition=%wide.region_5.6_spmd.clone, body=%wide.region_1.5_spmd.clone.sunk | while | flops 16823081984 | bytes 53471864 | solution.py:63
  96.9 22.6 %fusion.28 = (f32[512]{0:T(512)S(1)}, f32[512,4008]{0,1:T(8,128)S(1)}) fusion(bf16[4096,4008]{0,1:T(8,128)(2,1)} %get-tuple-element.681, bf16[2,512,4096]{2,1,0:T(8,128)(2,1)} %get-tuple-element.680, s32[]{:T(128)} %get-tuple-element.666), kind=kOutput, calls=%fused_computation.38.clone.1 | convolution fusion | flops 16812822528 | bytes 45238784 | tf_op jit(solution)/shard_map/while/body/eval_jaxpr/dot_general | solution.py:56
  119.5 2.2 select_reduce_fusion.2
  121.8 22.6 %fusion.28 = (f32[512]{0:T(512)S(1)}, f32[512,4008]{0,1:T(8,128)S(1)}) fusion(bf16[4096,4008]{0,1:T(8,128)(2,1)} %get-tuple-element.681, bf16[2,512,4096]{2,1,0:T(8,128)(2,1)} %get-tuple-element.680, s32[]{:T(128)} %get-tuple-element.666), kind=kOutput, calls=%fused_computation.38.clone.1 | convolution fusion | flops 16812822528 | bytes 45238784 | tf_op jit(solution)/shard_map/while/body/eval_jaxpr/dot_general | solution.py:56
  144.4 2.2 select_reduce_fusion.2
  147.3 3.4 all-to-all-start
  151.4 4.3 all-to-all-done
  155.7 3.9 all-to-all-start.1
  162.3 2.2 all-to-all-done.1
  164.5 3.9 all-to-all-start.2
  168.4 5.9 all-gather.4
  174.3 5.9 all-gather.5
  180.2 5.0 all-gather.3
  186.4 421.8 %while.65 = (s32[]{:T(128)}, f32[]{:T(128)}, f32[]{:T(128)}, f32[128]{0:T(128)S(1)}, f32[128]{0:T(128)S(1)}, /*index=5*/f32[128]{0:T(128)S(1)}, f32[128]{0:T(128)S(1)}, s32[]{:T(128)}, s32[]{:T(128)}) while((s32[]{:T(128)}, f32[]{:T(128)}, f32[]{:T(128)}, f32[128]{0:T(128)S(1)}, f32[128]{0:T(128)S(1)}, /*index=5*/f32[128]{0:T(128)S(1)}, ...), condition=%wide.region_12.13_spmd, body=%wide.region_11.12_spmd.sunk | while | flops 6 | bytes 189 | solution.py:107
  608.2 44.3 %while.66 = (s32[]{:T(128)}, f32[1]{0:T(128)}, f32[1]{0:T(128)S(1)}, f32[1]{0:T(128)S(1)}, s32[]{:T(128)}) while((s32[]{:T(128)}, f32[1]{0:T(128)}, f32[1]{0:T(128)S(1)}, f32[1]{0:T(128)S(1)}, s32[]{:T(128)}) %tuple.128), condition=%wide.region_14.15_spmd, body=%wide.region_13.14_spmd.sunk | while | flops 4 | bytes 141 | solution.py:120
  608.3 9.0 %collective-permute-start = (f32[1]{0:T(128)}, f32[1]{0:T(128)}, u32[]{:S(2)}, u32[]{:S(2)}) collective-permute-start(f32[1]{0:T(128)} %add.147), channel_id=1, source_target_pairs={{4,0},{8,4},{12,8},{16,12},{20,16},{24,20},{28,24},{5,1},{9,5},{13... | collective-permute-start | bytes 20 | tf_op jit(solution)/shard_map/while/body/eval_jaxpr/ppermute | solution.py:26
  619.8 2.9 collective-permute-start
  625.2 2.9 collective-permute-start
  630.7 2.9 collective-permute-start
  636.2 2.9 collective-permute-start
  641.7 2.9 collective-permute-start
  647.2 2.9 collective-permute-start
  (566 shorter events, 206.5 us)
Async XLA Ops:
  7.2 1.6 copy-start
  7.2 89.7 %all-gather.8.cloned.1.call-start = ((), (), s32[]{:S(2)}) async-start(), calls=%async_computation.3 | async-start | bytes 9437184 | tf_op jit(solution)/shard_map/all_gather | solution.py:50
  96.8 62.7 %copy-start.1 = (f32[128]{0:T(128)S(1)}, f32[128]{0:T(128)}, u32[]{:S(2)}) copy-start(f32[128]{0:T(128)} %param.22) | copy-start | bytes 1540
  96.8 88.4 %copy-start.2 = (f32[128]{0:T(128)S(1)}, f32[128]{0:T(128)}, u32[]{:S(2)}) copy-start(f32[128]{0:T(128)} %param.23) | copy-start | bytes 1540
  96.8 88.4 %copy-start.3 = (f32[128]{0:T(128)S(1)}, f32[128]{0:T(128)}, u32[]{:S(2)}) copy-start(f32[128]{0:T(128)} %param.24) | copy-start | bytes 1540
  96.8 88.4 %copy-start.4 = (s32[128]{0:T(128)S(1)}, s32[128]{0:T(128)}, u32[]{:S(2)}) copy-start(s32[128]{0:T(128)} %param.25) | copy-start | bytes 1540
  147.3 8.4 %all-to-all-start = ((f32[8,128,1]{1,2,0:T(1,128)}), f32[8,128,1]{1,2,0:T(1,128)S(1)}, u32[]{:S(2)}, u32[]{:S(2)}) async-start(f32[8,128,1]{1,2,0:T(1,128)} %all_to_all.18), calls=%async_computation | async-start | bytes 8192 | tf_op jit(solution)/shard_map/all_to_all | solution.py:74
  155.7 8.8 %all-to-all-start.1 = ((f32[8,128,1]{1,2,0:T(1,128)}), f32[8,128,1]{1,2,0:T(1,128)S(1)}, u32[]{:S(2)}, u32[]{:S(2)}) async-start(f32[8,128,1]{1,2,0:T(1,128)} %all_to_all.20), calls=%async_computation.1 | async-start | bytes 8192 | tf_op jit(solution)/shard_map/all_to_all | solution.py:75
  159.6 25.7 %collective-permute-start.1 = (f32[1]{0:T(128)S(1)}, f32[1]{0:T(128)}, u32[]{:S(2)}, u32[]{:S(2)}) collective-permute-start(f32[1]{0:T(128)S(1)} %bitcast.85), channel_id=1, source_target_pairs={{4,0},{8,4},{12,8},{16,12},{20,16},{24,20},{28,24},{5,1},{9,5},{13... | collective-permute-start | bytes 20 | tf_op jit(solution)/shard_map/ppermute | solution.py:26
  164.5 9.8 %all-to-all-start.2 = ((f32[8,128,1]{1,2,0:T(1,128)}), f32[8,128,1]{1,2,0:T(1,128)S(1)}, u32[]{:S(2)}, u32[]{:S(2)}) async-start(f32[8,128,1]{1,2,0:T(1,128)} %all_to_all.22), calls=%async_computation.2 | async-start | bytes 8192 | tf_op jit(solution)/shard_map/all_to_all | solution.py:76
  608.3 10.8 %collective-permute-start = (f32[1]{0:T(128)}, f32[1]{0:T(128)}, u32[]{:S(2)}, u32[]{:S(2)}) collective-permute-start(f32[1]{0:T(128)} %add.147), channel_id=1, source_target_pairs={{4,0},{8,4},{12,8},{16,12},{20,16},{24,20},{28,24},{5,1},{9,5},{13... | collective-permute-start | bytes 20 | tf_op jit(solution)/shard_map/while/body/eval_jaxpr/ppermute | solution.py:26
  619.8 4.8 collective-permute-start
  625.2 4.8 collective-permute-start
  630.7 4.8 collective-permute-start
  636.2 4.8 collective-permute-start
  641.7 4.8 collective-permute-start
  647.2 4.8 collective-permute-start
Sparse Core Ops, SparseCore 0:
  12.3 84.4 all-gather.7
where the time goes:
time: 664 us; the launch traced here: 660 us
  loops' own time  242 us (36%)
  local copies, waits for them, and re-layouts  187 us (28%)
  waiting for transfers between devices  104 us (16%)
  matrix products  48.5 us (7%)
  starting transfers between devices  39.4 us (6%)
  blocking collectives  16.7 us (3%)
  between operations  14.1 us (2%)
  other arithmetic  7.76 us (1%)
    another operation x1, loops' own time, per_device(): lax.scan(backward, (jnp.zeros((), jnp.float32), jnp.ones((), jnp.float32)...  237 us
    dynamic_slice x256, local copies, waits for them, and re-layouts, per_device(): lax.scan(backward, (jnp.zeros((), jnp.float32), jnp.ones((), jnp.float32)...  155 us
    all_gather x1, waiting for transfers between devices, per_device(): gathered = lax.all_gather(normed, 'batch', axis=0, tiled=True)  83.9 us
    dot_general x2, matrix products, score_block(): logits = jnp.dot(rows_block, unembed, preferred_element_type=jnp.float32)  45.2 us
    dynamic_update_slice x256, local copies, waits for them, and re-layouts, per_device(): lax.scan(backward, (jnp.zeros((), jnp.float32), jnp.ones((), jnp.float32)...  29.4 us
    ppermute x8, starting transfers between devices, from_behind(): lax.ppermute(value, axis, [(source, source + steps) for source in range(i...  28.2 us
    all_gather x3, blocking collectives, joined(): gathered = jax.tree.map(lambda a: lax.all_gather(a, axis), part)  16.7 us
    ppermute x8, waiting for transfers between devices, from_behind(): lax.ppermute(value, axis, [(source, source + steps) for source in range(i...  13.7 us
  transfers between devices with their start and end apart: 12, of which 10 were waited for; matrix products, arithmetic and copies ran while one was open for 0% of the time, Pallas kernels for 0%

commit v1 on v0

--- a/solution.py
+++ b/solution.py
@@ -7,6 +7,28 @@
 discount = 1.0
 trace_decay = 0.999
 penalty_weight = 0.1
+
+
+def joined_along(pieces, dim):
+    pieces = jnp.moveaxis(pieces, 0, dim)
+    shape = pieces.shape
+    return pieces.reshape(*shape[:dim], shape[dim] * shape[dim + 1], *shape[dim + 2 :])
+
+
+def gather_around(x, axis, dim):
+    count = lax.axis_size(axis)
+    pairs = [(i, (i + 1) % count) for i in range(count)]
+    back = [(b, a) for a, b in pairs]
+    lower, upper = ([], [])
+    for step in range(count - 1):
+        if step % 2 == 0:
+            lower.append(lax.ppermute(lower[-1] if lower else x, axis, pairs))
+        else:
+            upper.append(lax.ppermute(upper[-1] if upper else x, axis, back))
+    pieces = jnp.stack([*lower[::-1], x, *upper])
+    shift = lax.axis_index(axis) - len(lower)
+    pieces = pieces[(jnp.arange(count) - shift) % count]
+    return joined_along(pieces, dim)
 
 
 def joined(part, axis, combine):
@@ -47,7 +69,7 @@
     peers = lax.axis_size("batch")
     width = hidden.shape[1]
     normed = normalize(hidden, exit_layer, exit_gains)
-    gathered = lax.all_gather(normed, "batch", axis=0, tiled=True)
+    gathered = gather_around(normed, "batch", 0)
     block_rows = 512
     block_count = total_rows // block_rows
 

time: 664 us -> 694 us (1.045)
  starting transfers between devices: 39.4 us -> 76.8 us
  local copies, waits for them, and re-layouts: 187 us -> 213 us
  waiting for transfers between devices: 104 us -> 78.1 us
  between operations: 14.1 us -> 0.76 us
  loops' own time: 242 us -> 249 us
    all_gather x1 -> x0, waiting for transfers between devices: 83.9 us -> none  [per_device(): gathered = lax.all_gather(normed, 'batch', axis=0, tiled=True)]
    ppermute x0 -> x7, waiting for transfers between devices: none -> 56 us  [the longest x4 43.8 us: gather_around(): lower.append(lax.ppermute(lower[-1] if lower else x, axis, pairs))]
    all_to_all x1, starting transfers between devices: 3.43 us -> 23.9 us  [per_device(): lax.all_to_all(maxima, 'batch', split_axis=0, concat_axis=0, tiled=True)]
    ppermute x0 -> x7, starting transfers between devices: none -> 17.8 us  [the longest x4 10.3 us: gather_around(): lower.append(lax.ppermute(lower[-1] if lower else x, axis, pairs))]
    unnamed x10 -> x21, local copies, waits for them, and re-layouts: 0.02 us -> 12.5 us
    gather x0 -> x1, local copies, waits for them, and re-layouts: none -> 8.06 us  [gather_around(): pieces = pieces[(jnp.arange(count) - shift) % count]]
  transfers between devices with their start and end apart: 12 -> 18, of which waited for: 10 -> 16; matrix products, arithmetic and copies ran while one was open for 0% -> 2% of each run, Pallas kernels for 0% -> 0%
where the time goes in v1:
time: 694 us; the launch traced here: 690 us
  loops' own time  249 us (36%)
  local copies, waits for them, and re-layouts  213 us (31%)
  waiting for transfers between devices  78.1 us (11%)
  starting transfers between devices  76.8 us (11%)
  matrix products  47.5 us (7%)
  blocking collectives  16.6 us (2%)
  other arithmetic  7.78 us (1%)
    another operation x1, loops' own time, per_device(): lax.scan(backward, (jnp.zeros((), jnp.float32), jnp.ones((), jnp.float32)...  244 us
    dynamic_slice x256, local copies, waits for them, and re-layouts, per_device(): lax.scan(backward, (jnp.zeros((), jnp.float32), jnp.ones((), jnp.float32)...  160 us
    dot_general x2, matrix products, score_block(): logits = jnp.dot(rows_block, unembed, preferred_element_type=jnp.float32)  45.2 us
    ppermute x4, waiting for transfers between devices, gather_around(): lower.append(lax.ppermute(lower[-1] if lower else x, axis, pairs))  43.8 us
    dynamic_update_slice x256, local copies, waits for them, and re-layouts, per_device(): lax.scan(backward, (jnp.zeros((), jnp.float32), jnp.ones((), jnp.float32)...  29.4 us
    ppermute x8, starting transfers between devices, from_behind(): lax.ppermute(value, axis, [(source, source + steps) for source in range(i...  27.3 us
    all_to_all x1, starting transfers between devices, per_device(): lax.all_to_all(maxima, 'batch', split_axis=0, concat_axis=0, tiled=True)  23.9 us
    all_gather x3, blocking collectives, joined(): gathered = jax.tree.map(lambda a: lax.all_gather(a, axis), part)  16.6 us
  transfers between devices with their start and end apart: 18, of which 16 were waited for; matrix products, arithmetic and copies ran while one was open for 2% of the time, Pallas kernels for 0%

profile of v1, /device:TPU:1, one launch (start us, length us, event | category | flops | bytes accessed | tf_op | source)
XLA Modules:
  0.0 689.9 jit_solution(4344166199350828798)
XLA Ops:
  4.5 2.7 collective-permute-start.1
  7.3 11.7 %collective-permute-done.1 = bf16[128,4096]{1,0:T(8,128)(2,1)S(1)} collective-permute-done((bf16[128,4096]{1,0:T(8,128)(2,1)S(1)}, bf16[128,4096]{1,0:T(8,128)(2,1)S(1)}, u32[]{:S(2)}, u32[]{:S(2)}) %collective-permute-start.1) | collective-permute-done | bytes 1048608 | tf_op jit(solution)/shard_map/ppermute | solution.py:25
  21.6 19.0 %collective-permute-done.2 = bf16[128,4096]{1,0:T(8,128)(2,1)S(1)} collective-permute-done((bf16[128,4096]{1,0:T(8,128)(2,1)S(1)}, bf16[128,4096]{1,0:T(8,128)(2,1)S(1)}, u32[]{:S(2)}, u32[]{:S(2)}) %collective-permute-start.2) | collective-permute-done | bytes 1048608 | tf_op jit(solution)/shard_map/ppermute | solution.py:25
  43.1 3.7 collective-permute-done.5
  49.1 10.1 %collective-permute-done.3 = bf16[128,4096]{1,0:T(8,128)(2,1)} collective-permute-done((bf16[128,4096]{1,0:T(8,128)(2,1)S(1)}, bf16[128,4096]{1,0:T(8,128)(2,1)}, u32[]{:S(2)}, u32[]{:S(2)}) %collective-permute-start.3) | collective-permute-done | bytes 1048608 | tf_op jit(solution)/shard_map/ppermute | solution.py:25
  62.5 7.8 %collective-permute-done.6 = bf16[128,4096]{1,0:T(8,128)(2,1)} collective-permute-done((bf16[128,4096]{1,0:T(8,128)(2,1)S(1)}, bf16[128,4096]{1,0:T(8,128)(2,1)}, u32[]{:S(2)}, u32[]{:S(2)}) %collective-permute-start.6) | collective-permute-done | bytes 1048608 | tf_op jit(solution)/shard_map/ppermute | solution.py:27
  70.3 5.1 collective-permute-start.7
  75.4 2.9 collective-permute-done.4
  92.6 8.1 %gather_fusion = bf16[8,128,4096]{2,1,0:T(8,128)(2,1)} fusion(bf16[8,128,4096]{2,1,0:T(8,128)(2,1)} %bitcast_dynamic-update-slice_fusion, s32[1024]{0:T(1024)S(1)} %pad_clamp_fusion), kind=kCustom, calls=%fused_computation | custom fusion | bytes 16777248 | tf_op jit(solution)/shard_map/gather | solution.py:30
  100.7 49.9 %while.67 = (s32[]{:T(128)}, f32[2,512]{1,0:T(2,128)S(1)}, f32[2,512]{1,0:T(2,128)S(1)}, f32[2,512]{1,0:T(2,128)S(1)}, bf16[2,512,4096]{2,1,0:T(8,128)(2,1)}, /*...) while((s32[]{:T(128)}, f32[2,512]{1,0:T(2,128)S(1)}, ...), condition=%wide.region_5.6_spmd.clone, body=%wide.region_1.5_spmd.clone.sunk | while | flops 16823081984 | bytes 53471864 | solution.py:85
  100.7 22.6 %fusion.30 = (f32[512]{0:T(512)S(1)}, f32[512,4008]{0,1:T(8,128)S(1)}) fusion(bf16[4096,4008]{0,1:T(8,128)(2,1)} %get-tuple-element.681, bf16[2,512,4096]{2,1,0:T(8,128)(2,1)} %get-tuple-element.680, s32[]{:T(128)} %get-tuple-element.666), kind=kOutput, calls=%fused_computation.54.clone.1 | convolution fusion | flops 16812822528 | bytes 45238784 | tf_op jit(solution)/shard_map/while/body/eval_jaxpr/dot_general | solution.py:78
  125.6 22.6 %fusion.30 = (f32[512]{0:T(512)S(1)}, f32[512,4008]{0,1:T(8,128)S(1)}) fusion(bf16[4096,4008]{0,1:T(8,128)(2,1)} %get-tuple-element.681, bf16[2,512,4096]{2,1,0:T(8,128)(2,1)} %get-tuple-element.680, s32[]{:T(128)} %get-tuple-element.666), kind=kOutput, calls=%fused_computation.54.clone.1 | convolution fusion | flops 16812822528 | bytes 45238784 | tf_op jit(solution)/shard_map/while/body/eval_jaxpr/dot_general | solution.py:78
  151.2 23.9 %all-to-all-start = ((f32[8,128,1]{1,2,0:T(1,128)}), f32[8,128,1]{1,2,0:T(1,128)S(1)}, u32[]{:S(2)}, u32[]{:S(2)}) async-start(f32[8,128,1]{1,2,0:T(1,128)} %all_to_all.18), calls=%async_computation | async-start | bytes 8192 | tf_op jit(solution)/shard_map/all_to_all | solution.py:96
  175.6 4.3 all-to-all-done
  180.0 3.9 all-to-all-start.1
  188.8 3.9 all-to-all-start.2
  192.7 5.8 all-gather.4
  198.5 5.9 all-gather.5
  204.4 4.9 all-gather.3
  210.6 432.9 %while.65 = (s32[]{:T(128)}, f32[]{:T(128)}, f32[]{:T(128)}, f32[128]{0:T(128)S(1)}, f32[128]{0:T(128)S(1)}, /*index=5*/f32[128]{0:T(128)S(1)}, f32[128]{0:T(128)S(1)}, s32[]{:T(128)}, s32[]{:T(128)}) while((s32[]{:T(128)}, f32[]{:T(128)}, f32[]{:T(128)}, f32[128]{0:T(128)S(1)}, f32[128]{0:T(128)S(1)}, /*index=5*/f32[128]{0:T(128)S(1)}, ...), condition=%wide.region_12.13_spmd, body=%wide.region_11.12_spmd.sunk | while | flops 6 | bytes 189 | solution.py:129
  643.5 45.8 %while.66 = (s32[]{:T(128)}, f32[1]{0:T(128)}, f32[1]{0:T(128)S(1)}, f32[1]{0:T(128)S(1)}, s32[]{:T(128)}) while((s32[]{:T(128)}, f32[1]{0:T(128)}, f32[1]{0:T(128)S(1)}, f32[1]{0:T(128)S(1)}, s32[]{:T(128)}) %tuple.127), condition=%wide.region_14.15_spmd, body=%wide.region_13.14_spmd.sunk | while | flops 4 | bytes 141 | solution.py:142
  643.6 8.9 %collective-permute-start = (f32[1]{0:T(128)}, f32[1]{0:T(128)}, u32[]{:S(2)}, u32[]{:S(2)}) collective-permute-start(f32[1]{0:T(128)} %add.181), channel_id=1, source_target_pairs={{4,0},{8,4},{12,8},{16,12},{20,16},{24,20},{28,24},{5,1},{9,5},{13... | collective-permute-start | bytes 20 | tf_op jit(solution)/shard_map/while/body/eval_jaxpr/ppermute | solution.py:48
  655.3 2.7 collective-permute-start
  661.0 2.7 collective-permute-start
  (592 shorter events, 257.0 us)
Async XLA Ops:
  4.5 14.5 %collective-permute-start.1 = (bf16[128,4096]{1,0:T(8,128)(2,1)S(1)}, bf16[128,4096]{1,0:T(8,128)(2,1)S(1)}, u32[]{:S(2)}, u32[]{:S(2)}) collective-permute-start(bf16[128,4096]{1,0:T(8,128)(2,1)S(1)} %fusion.13), channel_id=1, source_target_pairs={{0,4},{4,8},{8,12},{12,16},{16,20},{20,24},{24,28},{28,0},{1,5},{5... | collective-permute-start | bytes 3145736 | tf_op jit(solution)/shard_map/ppermute | solution.py:25
  19.0 21.6 %collective-permute-start.2 = (bf16[128,4096]{1,0:T(8,128)(2,1)S(1)}, bf16[128,4096]{1,0:T(8,128)(2,1)S(1)}, u32[]{:S(2)}, u32[]{:S(2)}) collective-permute-start(bf16[128,4096]{1,0:T(8,128)(2,1)S(1)} %collective-permute-done.1), channel_id=1, source_target_pairs={{0,4},{4,8},{8,12},{12,16},{16,20},{20,24},{24,28},{28,0},{1,5},{5... | collective-permute-start | bytes 3145736 | tf_op jit(solution)/shard_map/ppermute | solution.py:25
  21.5 25.3 %collective-permute-start.5 = (bf16[128,4096]{1,0:T(8,128)(2,1)S(1)}, bf16[128,4096]{1,0:T(8,128)(2,1)S(1)}, u32[]{:S(2)}, u32[]{:S(2)}) collective-permute-start(bf16[128,4096]{1,0:T(8,128)(2,1)S(1)} %fusion.13), channel_id=1, source_target_pairs={{4,0},{8,4},{12,8},{16,12},{20,16},{24,20},{28,24},{0,28},{5,1},{9... | collective-permute-start | bytes 3145736 | tf_op jit(solution)/shard_map/ppermute | solution.py:27
  40.6 6.2 copy-start.2
  40.6 18.6 %collective-permute-start.3 = (bf16[128,4096]{1,0:T(8,128)(2,1)S(1)}, bf16[128,4096]{1,0:T(8,128)(2,1)}, u32[]{:S(2)}, u32[]{:S(2)}) collective-permute-start(bf16[128,4096]{1,0:T(8,128)(2,1)S(1)} %collective-permute-done.2), channel_id=1, source_target_pairs={{0,4},{4,8},{8,12},{12,16},{16,20},{20,24},{24,28},{28,0},{1,5},{5... | collective-permute-start | bytes 3145736 | tf_op jit(solution)/shard_map/ppermute | solution.py:25
  46.8 23.5 %collective-permute-start.6 = (bf16[128,4096]{1,0:T(8,128)(2,1)S(1)}, bf16[128,4096]{1,0:T(8,128)(2,1)}, u32[]{:S(2)}, u32[]{:S(2)}) collective-permute-start(bf16[128,4096]{1,0:T(8,128)(2,1)S(1)} %collective-permute-done.5), channel_id=1, source_target_pairs={{4,0},{8,4},{12,8},{16,12},{20,16},{24,20},{28,24},{0,28},{5,1},{9... | collective-permute-start | bytes 3145736 | tf_op jit(solution)/shard_map/ppermute | solution.py:27
  59.2 19.2 %collective-permute-start.4 = (bf16[128,4096]{1,0:T(8,128)(2,1)}, bf16[128,4096]{1,0:T(8,128)(2,1)}, u32[]{:S(2)}, u32[]{:S(2)}) collective-permute-start(bf16[128,4096]{1,0:T(8,128)(2,1)} %collective-permute-done.3), channel_id=1, source_target_pairs={{0,4},{4,8},{8,12},{12,16},{16,20},{20,24},{24,28},{28,0},{1,5},{5... | collective-permute-start | bytes 3145736 | tf_op jit(solution)/shard_map/ppermute | solution.py:25
  70.3 21.2 %collective-permute-start.7 = (bf16[128,4096]{1,0:T(8,128)(2,1)}, bf16[128,4096]{1,0:T(8,128)(2,1)S(1)}, u32[]{:S(2)}, u32[]{:S(2)}) collective-permute-start(bf16[128,4096]{1,0:T(8,128)(2,1)} %collective-permute-done.6), channel_id=1, source_target_pairs={{4,0},{8,4},{12,8},{16,12},{20,16},{24,20},{28,24},{0,28},{5,1},{9... | collective-permute-start | bytes 3145736 | tf_op jit(solution)/shard_map/ppermute | solution.py:27
  100.6 83.2 %copy-start.3 = (f32[128]{0:T(128)S(1)}, f32[128]{0:T(128)}, u32[]{:S(2)}) copy-start(f32[128]{0:T(128)} %param.22) | copy-start | bytes 1540
  100.6 108.8 %copy-start.4 = (f32[128]{0:T(128)S(1)}, f32[128]{0:T(128)}, u32[]{:S(2)}) copy-start(f32[128]{0:T(128)} %param.23) | copy-start | bytes 1540
  100.6 108.8 %copy-start.5 = (f32[128]{0:T(128)S(1)}, f32[128]{0:T(128)}, u32[]{:S(2)}) copy-start(f32[128]{0:T(128)} %param.24) | copy-start | bytes 1540
  100.7 108.8 %copy-start.6 = (s32[128]{0:T(128)S(1)}, s32[128]{0:T(128)}, u32[]{:S(2)}) copy-start(s32[128]{0:T(128)} %param.25) | copy-start | bytes 1540
  150.5 539.4 %copy-start.1 = (f32[8,4096]{1,0:T(8,128)S(1)}, f32[8,4096]{1,0:T(8,128)}, u32[]{:S(2)}) copy-start(f32[8,4096]{1,0:T(8,128)} %param.19) | copy-start | bytes 393220
  151.2 28.8 %all-to-all-start = ((f32[8,128,1]{1,2,0:T(1,128)}), f32[8,128,1]{1,2,0:T(1,128)S(1)}, u32[]{:S(2)}, u32[]{:S(2)}) async-start(f32[8,128,1]{1,2,0:T(1,128)} %all_to_all.18), calls=%async_computation | async-start | bytes 8192 | tf_op jit(solution)/shard_map/all_to_all | solution.py:96
  180.0 8.8 %all-to-all-start.1 = ((f32[8,128,1]{1,2,0:T(1,128)}), f32[8,128,1]{1,2,0:T(1,128)S(1)}, u32[]{:S(2)}, u32[]{:S(2)}) async-start(f32[8,128,1]{1,2,0:T(1,128)} %all_to_all.20), calls=%async_computation.1 | async-start | bytes 8192 | tf_op jit(solution)/shard_map/all_to_all | solution.py:97
  183.9 25.6 %collective-permute-start.8 = (f32[1]{0:T(128)S(1)}, f32[1]{0:T(128)}, u32[]{:S(2)}, u32[]{:S(2)}) collective-permute-start(f32[1]{0:T(128)S(1)} %bitcast.104), channel_id=1, source_target_pairs={{4,0},{8,4},{12,8},{16,12},{20,16},{24,20},{28,24},{5,1},{9,5},{13... | collective-permute-start | bytes 20 | tf_op jit(solution)/shard_map/ppermute | solution.py:48
  188.8 9.7 %all-to-all-start.2 = ((f32[8,128,1]{1,2,0:T(1,128)}), f32[8,128,1]{1,2,0:T(1,128)S(1)}, u32[]{:S(2)}, u32[]{:S(2)}) async-start(f32[8,128,1]{1,2,0:T(1,128)} %all_to_all.22), calls=%async_computation.2 | async-start | bytes 8192 | tf_op jit(solution)/shard_map/all_to_all | solution.py:98
  643.6 11.0 %collective-permute-start = (f32[1]{0:T(128)}, f32[1]{0:T(128)}, u32[]{:S(2)}, u32[]{:S(2)}) collective-permute-start(f32[1]{0:T(128)} %add.181), channel_id=1, source_target_pairs={{4,0},{8,4},{12,8},{16,12},{20,16},{24,20},{28,24},{5,1},{9,5},{13... | collective-permute-start | bytes 20 | tf_op jit(solution)/shard_map/while/body/eval_jaxpr/ppermute | solution.py:48
  655.3 5.0 collective-permute-start
  661.0 5.0 collective-permute-start
  666.7 5.0 collective-permute-start
  672.4 5.0 collective-permute-start
  678.1 5.0 collective-permute-start
  683.8 5.0 collective-permute-start
  (1 other events, 1.6 us)
